TPU v7x, 32 devices: a whole 2x2x4 slice. The times are simulated.
32 devices in a mesh: group: 2 (over x), seq: 16 (over z, y, core).
Axes of the slice: x: 2, y: 2, z: 4, core: 2. Of those that a mesh axis runs over, the one named last changes fastest.
Arguments:
- hidden: bfloat16 [8, 256, 1408], P('group', 'seq'), parts along dimension 0, may hold values from -14 to 14
- skip: bfloat16 [8, 256, 1408], P('group', 'seq'), parts along dimension 0, may hold values from -6 to 6
- timestep: int32 [8], P('group'), parts along dimension 0, may hold values from 0 to 999
- w_skip: bfloat16 [2816, 1408], P('seq'), may hold values from -0.109375 to 0.109375
- w_mod: bfloat16 [256, 4224], replicated, may hold values from -5 to 5
- w_qkv: bfloat16 [1408, 4224], P('seq'), may hold values from -0.15625 to 0.15625
- w_out: bfloat16 [1408, 1408], P('seq'), may hold values from -0.15625 to 0.15625
Outputs:
- result: bfloat16 [8, 256, 1408], P('group', 'seq'), parts along dimension 0
There are 2 independent parts, one for each index of `group`. A program takes and returns all parts, laid end to end along the dimension named above; an argument that names none is the same for every part. Nothing has to cross between parts.
All inputs are finite; a program needn't handle non-finite values.
Results may differ from a plain program's by a relative error of at most 0.0095.
Values may be sent and summed in bfloat16 or wider, within the bound.
A program may use at most 128 MiB of HBM per device.

v0:
```python
import math

import jax
import jax.numpy as jnp
from jax import lax
from jax.sharding import PartitionSpec as P

H = 16
HD = 88
TDIM = 256


def layer_norm(x):
    mean = jnp.mean(x, axis=-1, keepdims=True)
    var = jnp.mean((x - mean) ** 2, axis=-1, keepdims=True)
    return (x - mean) * lax.rsqrt(var + 1e-06)


def attend_pair(trio):
    qpair, kpair, vpair = trio
    length = qpair.shape[0]
    block = min(512, length)
    qblocks = qpair.reshape(length // block, block, qpair.shape[1])

    def one_block(qblk):
        scores = jnp.einsum("qd,kd->qk", qblk, kpair, preferred_element_type=jnp.float32)
        probs = jax.nn.softmax(scores, axis=-1).astype(jnp.bfloat16)
        return jnp.dot(probs, vpair, preferred_element_type=jnp.float32).astype(jnp.bfloat16)

    return lax.map(one_block, qblocks).reshape(length, qpair.shape[1])


def to_heads(x, seqs, local):
    return jnp.transpose(x, (0, 2, 1, 3)).reshape(seqs * H, local, HD)


def per_device(hidden, skip, timestep, w_skip, w_mod, w_qkv, w_out):
    seqs, local, width = hidden.shape
    tok_rows = seqs * local
    combined = jnp.concatenate([hidden, skip], axis=2).reshape(tok_rows, 2 * width)
    full_skip = lax.all_gather(w_skip, "seq", axis=0, tiled=True)
    merged = jnp.dot(combined, full_skip, preferred_element_type=jnp.float32).astype(jnp.bfloat16)
    half = TDIM // 2
    freqs = jnp.exp(-math.log(10000.0) * jnp.arange(half, dtype=jnp.float32) / half)
    angles = timestep.astype(jnp.float32)[:, None] * freqs[None, :]
    embed = jnp.concatenate([jnp.cos(angles), jnp.sin(angles)], axis=1)
    act = jax.nn.silu(embed).astype(jnp.bfloat16)
    mod = jnp.dot(act, w_mod, preferred_element_type=jnp.float32)
    shift, scale, gate = (mod[:, :width], mod[:, width : 2 * width], mod[:, 2 * width :])
    base = merged.astype(jnp.float32).reshape(seqs, local, width)
    normed = (layer_norm(base) * (1.0 + scale[:, None, :]) + shift[:, None, :]).astype(jnp.bfloat16)
    normed = normed.reshape(tok_rows, width)
    full_qkv = lax.all_gather(w_qkv, "seq", axis=0, tiled=True)
    qkv = jnp.dot(normed, full_qkv, preferred_element_type=jnp.float32)
    qkv = qkv.reshape(seqs, local, 3, H, HD)
    query = (layer_norm(qkv[:, :, 0]) * HD ** (-0.5)).astype(jnp.bfloat16)
    key = layer_norm(qkv[:, :, 1]).astype(jnp.bfloat16)
    value = qkv[:, :, 2].astype(jnp.bfloat16)
    query = to_heads(query, seqs, local)
    key = to_heads(key, seqs, local)
    value = to_heads(value, seqs, local)
    query, key, value = (
        lax.all_to_all(query, "seq", split_axis=0, concat_axis=1, tiled=True),
        lax.all_to_all(key, "seq", split_axis=0, concat_axis=1, tiled=True),
        lax.all_to_all(value, "seq", split_axis=0, concat_axis=1, tiled=True),
    )
    attended = lax.map(attend_pair, (query, key, value))
    attended = lax.all_to_all(attended, "seq", split_axis=1, concat_axis=0, tiled=True)
    attended = jnp.transpose(attended.reshape(seqs, H, local, HD), (0, 2, 1, 3)).reshape(
        tok_rows, width
    )
    full_out = lax.all_gather(w_out, "seq", axis=0, tiled=True)
    projected = jnp.dot(attended, full_out, preferred_element_type=jnp.float32)
    projected = projected.reshape(seqs, local, width)
    return (base + gate[:, None, :] * projected).astype(jnp.bfloat16)


def solution(mesh):
    placed = (
        P("group", "seq", None),
        P("group", "seq", None),
        P("group"),
        P("seq", None),
        P(),
        P("seq", None),
        P("seq", None),
    )
    return jax.shard_map(
        per_device, mesh=mesh, in_specs=placed, out_specs=P("group", "seq", None), check_vma=False
    )
```

profile of v0, /device:TPU:0, one launch (start us, length us, event | category | flops | bytes accessed | tf_op | source)
XLA Modules:
  0.0 280.8 jit_solution(14518361080193916510)
XLA Ops:
  6.5 0.7 all-gather.4.cloned.1.call-update
  7.3 0.7 all-gather.6.cloned.1.call-update
  8.1 0.7 all-gather.8.cloned.1.call-update
  8.8 0.7 convert_element_type.39
  9.4 1.0 pad_maximum_fusion
  10.6 0.4 fusion.28
  11.0 72.7 %all-gather.4.cloned.1.call-done = bf16[2816,1408]{1,0:T(8,128)(2,1)} async-done(((bf16[176,1408]{1,0:T(8,128)(2,1)}), bf16[2816,1408]{1,0:T(8,128)(2,1)}) %all-gather.4.cloned.1.call-update) | async-done | bytes 7929872 | tf_op jit(solution)/shard_map/all_gather | solution.py:41
  83.7 4.8 %fusion.35 = (f32[64]{0:T(128)S(1)}, f32[64,1408]{1,0:T(8,128)S(1)}) fusion(bf16[64,2816]{1,0:T(8,128)(2,1)S(1)} %bitcast.105, bf16[2816,1408]{1,0:T(8,128)(2,1)} %all-gather.4.cloned.1.call-done), kind=kOutput, calls=%fused_computation.57 | convolution fusion | flops 507781056 | bytes 8651008 | tf_op jit(solution)/shard_map/dot_general | solution.py:42
  88.9 91.9 %all-gather.6.cloned.1.call-done = bf16[1408,4224]{1,0:T(8,128)(2,1)} async-done(((bf16[88,4224]{1,0:T(8,128)(2,1)}), bf16[1408,4224]{1,0:T(8,128)(2,1)}) %all-gather.6.cloned.1.call-update) | async-done | bytes 11894800 | tf_op jit(solution)/shard_map/all_gather | solution.py:53
  180.7 16.3 %copy.19 = bf16[4224,1408]{1,0:T(8,128)(2,1)} copy(bf16[4224,1408]{0,1:T(8,128)(2,1)} %bitcast.102) | data formatting | bytes 23789568 | tf_op jit(solution)/shard_map/dot_general | solution.py:54
  197.0 7.9 %fusion.36 = f32[4,16,3,16,88]{4,1,3,2,0:T(8,128)S(1)} fusion(bf16[4,16,1408,1,1]{2,1,4,3,0:T(8,128)(2,1)S(1)} %bitcast.114, bf16[3,16,88,1408,1]{3,2,1,0,4:T(8,128)(2,1)} %bitcast.103), kind=kOutput, calls=%fused_computation.58 | convolution fusion | flops 761266176 | bytes 13156352 | tf_op jit(solution)/shard_map/dot_general | solution.py:54
  204.9 0.3 slice_reduce_fusion
  205.2 0.6 multiply_reduce_fusion
  206.0 1.3 multiply_convert_fusion
  207.3 17.3 %all_to_all.69 = bf16[64,16,88]{2,1,0:T(8,128)(2,1)S(1)} all-to-all(bf16[64,16,88]{2,1,0:T(8,128)(2,1)S(1)} %bitcast.112), channel_id=1, replica_groups=mesh['group'=2,'seq'=16] {'seq'}, dimensions={0} | all-to-all | bytes 360448 | tf_op jit(solution)/shard_map/all_to_all | solution.py:63
  224.7 5.4 %all-to-all-start.1 = ((bf16[64,16,88]{2,1,0:T(8,128)(2,1)}), bf16[64,16,88]{2,1,0:T(8,128)(2,1)S(1)}, u32[]{:S(2)}, u32[]{:S(2)}) async-start(bf16[64,16,88]{2,1,0:T(8,128)(2,1)} %bitcast.22), calls=%async_computation.1 | async-start | bytes 524288 | tf_op jit(solution)/shard_map/all_to_all | solution.py:64
  230.1 1.8 slice.39
  231.9 8.2 %all-to-all-done.1 = bf16[64,16,88]{2,1,0:T(8,128)(2,1)S(1)} async-done(((bf16[64,16,88]{2,1,0:T(8,128)(2,1)}), bf16[64,16,88]{2,1,0:T(8,128)(2,1)S(1)}, u32[]{:S(2)}, u32[]{:S(2)}) %all-to-all-start.1) | async-done | bytes 180256 | tf_op jit(solution)/shard_map/all_to_all | solution.py:64
  240.1 4.2 %all-to-all-start.2 = ((bf16[64,16,88]{2,1,0:T(8,128)(2,1)}), bf16[64,16,88]{2,1,0:T(8,128)(2,1)}, u32[]{:S(2)}, u32[]{:S(2)}) async-start(bf16[64,16,88]{2,1,0:T(8,128)(2,1)} %bitcast.28), calls=%async_computation.2 | async-start | bytes 524288 | tf_op jit(solution)/shard_map/all_to_all | solution.py:65
  244.4 10.0 %all-to-all-done.2 = bf16[64,16,88]{2,1,0:T(8,128)(2,1)} async-done(((bf16[64,16,88]{2,1,0:T(8,128)(2,1)}), bf16[64,16,88]{2,1,0:T(8,128)(2,1)}, u32[]{:S(2)}, u32[]{:S(2)}) %all-to-all-start.2) | async-done | bytes 180256 | tf_op jit(solution)/shard_map/all_to_all | solution.py:65
  254.3 1.0 copy.22
  255.3 2.1 while.10
  257.6 12.7 %all_to_all.70 = bf16[4,256,88]{2,0,1:T(4,128)(2,1)S(1)} all-to-all(bf16[4,256,88]{2,0,1:T(4,128)(2,1)S(1)} %copy.23), channel_id=1, replica_groups=mesh['group'=2,'seq'=16] {'seq'}, dimensions={1} | all-to-all | bytes 360448 | tf_op jit(solution)/shard_map/all_to_all | solution.py:68
  270.8 3.5 %fusion.22 = bf16[4,16,1408]{2,1,0:T(8,128)(2,1)} fusion(f32[4,16,1408]{2,1,0:T(8,128)S(1)} %bitcast.104, bf16[4,16,1408]{2,1,0:T(8,128)(2,1)S(1)} %dot_general.34, bf16[1408,1408]{1,0:T(8,128)(2,1)} %all-gather.8.cloned.1.call-done, f32[4,1408]{1,0:T(4,128)S(1)} %get-tuple-element.66), kind=kOutput, calls=%fused_computation.21 | convolution fusion | flops 254025728 | bytes 4708352 | tf_op jit(solution)/shard_map/dot_general | solution.py:73
  (38 shorter events, 3.4 us)
Async XLA Ops:
  6.5 4.0 %copy-start = (bf16[256,4224]{1,0:T(8,128)(2,1)S(1)}, bf16[256,4224]{1,0:T(8,128)(2,1)}, u32[]{:S(2)}) copy-start(bf16[256,4224]{1,0:T(8,128)(2,1)} %param.13) | copy-start | bytes 6488068
  6.5 77.1 %all-gather.4.cloned.1.call-start = ((), (), s32[]{:S(2)}) async-start(), calls=%async_computation.4 | async-start | bytes 8425472 | tf_op jit(solution)/shard_map/all_gather | solution.py:41
  7.3 173.5 %all-gather.6.cloned.1.call-start = ((), (), s32[]{:S(2)}) async-start(), calls=%async_computation.5 | async-start | bytes 12638208 | tf_op jit(solution)/shard_map/all_gather | solution.py:53
  8.0 262.8 %all-gather.8.cloned.1.call-start = ((), (), s32[]{:S(2)}) async-start(), calls=%async_computation.6 | async-start | bytes 4212736 | tf_op jit(solution)/shard_map/all_gather | solution.py:72
  204.9 1.2 copy-start.1
  224.7 15.5 %all-to-all-start.1 = ((bf16[64,16,88]{2,1,0:T(8,128)(2,1)}), bf16[64,16,88]{2,1,0:T(8,128)(2,1)S(1)}, u32[]{:S(2)}, u32[]{:S(2)}) async-start(bf16[64,16,88]{2,1,0:T(8,128)(2,1)} %bitcast.22), calls=%async_computation.1 | async-start | bytes 524288 | tf_op jit(solution)/shard_map/all_to_all | solution.py:64
  240.1 14.2 %all-to-all-start.2 = ((bf16[64,16,88]{2,1,0:T(8,128)(2,1)}), bf16[64,16,88]{2,1,0:T(8,128)(2,1)}, u32[]{:S(2)}, u32[]{:S(2)}) async-start(bf16[64,16,88]{2,1,0:T(8,128)(2,1)} %bitcast.28), calls=%async_computation.2 | async-start | bytes 524288 | tf_op jit(solution)/shard_map/all_to_all | solution.py:65
Sparse Core Ops, SparseCore 0:
  9.5 74.1 all-gather.3
  85.8 94.8 all-gather.5
  182.9 50.8 all-gather.7
where the time goes:
time: 282 us; the launch traced here: 281 us
  waiting for transfers between devices  185 us (66%)
  blocking collectives  30 us (11%)
  local copies, waits for them, and re-layouts  19.7 us (7%)
  matrix products  18.3 us (6%)
  between operations  13.3 us (5%)
  starting transfers between devices  9.72 us (3%)
  other arithmetic  4.83 us (2%)
    all_gather x1, waiting for transfers between devices, per_device(): full_qkv = lax.all_gather(w_qkv, 'seq', axis=0, tiled=True)  91.9 us
    all_gather x1, waiting for transfers between devices, per_device(): full_skip = lax.all_gather(w_skip, 'seq', axis=0, tiled=True)  72.7 us
    all_to_all x1, blocking collectives, per_device(): lax.all_to_all(query, 'seq', split_axis=0, concat_axis=1, tiled=True)  17.3 us
    dot_general x1, local copies, waits for them, and re-layouts, per_device(): qkv = jnp.dot(normed, full_qkv, preferred_element_type=jnp.float32)  16.3 us
    all_to_all x1, blocking collectives, per_device(): lax.all_to_all(attended, 'seq', split_axis=1, concat_axis=0, tiled=True)  12.7 us
    all_to_all x1, waiting for transfers between devices, per_device(): lax.all_to_all(value, 'seq', split_axis=0, concat_axis=1, tiled=True)  9.96 us
    all_to_all x1, waiting for transfers between devices, per_device(): lax.all_to_all(key, 'seq', split_axis=0, concat_axis=1, tiled=True)  8.23 us
    dot_general x1, matrix products, per_device(): qkv = jnp.dot(normed, full_qkv, preferred_element_type=jnp.float32)  7.86 us
  transfers between devices with their start and end apart: 5, of which 4 were waited for; matrix products, arithmetic and copies ran while one was open for 14% of the time, Pallas kernels for 0%

commit v1 on v0

--- a/solution.py
+++ b/solution.py
@@ -1,3 +1,4 @@
+import functools
 import math
 
 import jax
@@ -34,7 +35,7 @@
     return jnp.transpose(x, (0, 2, 1, 3)).reshape(seqs * H, local, HD)
 
 
-def per_device(hidden, skip, timestep, w_skip, w_mod, w_qkv, w_out):
+def gathered(hidden, skip, timestep, w_skip, w_mod, w_qkv, w_out):
     seqs, local, width = hidden.shape
     tok_rows = seqs * local
     combined = jnp.concatenate([hidden, skip], axis=2).reshape(tok_rows, 2 * width)
@@ -75,7 +76,50 @@
     return (base + gate[:, None, :] * projected).astype(jnp.bfloat16)
 
 
+def modulation(timestep, w_mod):
+    half = TDIM // 2
+    freqs = jnp.exp(-math.log(10000.0) * jnp.arange(half, dtype=jnp.float32) / half)
+    angles = timestep.astype(jnp.float32)[:, None] * freqs[None, :]
+    embed = jnp.concatenate([jnp.cos(angles), jnp.sin(angles)], axis=1)
+    act = jax.nn.silu(embed).astype(jnp.bfloat16)
+    return jnp.dot(act, w_mod, preferred_element_type=jnp.float32)
+
+
+def head_split(n, hidden, skip, timestep, w_skip, w_mod, w_qkv, w_out):
+    seqs, local, width = hidden.shape
+    rows = seqs * local
+    heads = H // n
+    combined = jnp.concatenate([hidden, skip], axis=2).reshape(rows, 2 * width)
+    spread = lax.all_to_all(combined, "seq", split_axis=1, concat_axis=0, tiled=True)
+    wq = w_qkv.reshape(w_qkv.shape[0], 3, n, heads * HD)
+    wq = lax.all_to_all(wq, "seq", split_axis=2, concat_axis=0, tiled=True)
+    wq = wq.reshape(width, 3 * heads * HD)
+    part = jnp.dot(spread, w_skip, preferred_element_type=jnp.float32).astype(jnp.bfloat16)
+    merged = lax.psum_scatter(part, "seq", scatter_dimension=0, tiled=True)
+    mod = modulation(timestep, w_mod)
+    shift, scale, gate = (mod[:, :width], mod[:, width : 2 * width], mod[:, 2 * width :])
+    base = merged.astype(jnp.float32).reshape(seqs, local, width)
+    normed = (layer_norm(base) * (1.0 + scale[:, None, :]) + shift[:, None, :]).astype(jnp.bfloat16)
+    every = lax.all_gather(normed.reshape(rows, width), "seq", axis=0, tiled=True)
+    qkv = jnp.dot(every, wq, preferred_element_type=jnp.float32)
+    qkv = qkv.reshape(n, seqs, local, 3, heads, HD)
+    query = (layer_norm(qkv[:, :, :, 0]) * HD ** (-0.5)).astype(jnp.bfloat16)
+    key = layer_norm(qkv[:, :, :, 1]).astype(jnp.bfloat16)
+    value = qkv[:, :, :, 2].astype(jnp.bfloat16)
+    scores = jnp.einsum("mslhd,ntshd->shmlnt".replace("ntshd", "nsthd"), query, key, preferred_element_type=jnp.float32)
+    shape = scores.shape
+    probs = jax.nn.softmax(scores.reshape(shape[:4] + (-1,)), axis=-1).astype(jnp.bfloat16).reshape(shape)
+    attended = jnp.einsum("shmlnt,nsthd->mslhd", probs, value, preferred_element_type=jnp.float32)
+    attended = attended.astype(jnp.bfloat16).reshape(n * rows, heads * HD)
+    part = jnp.dot(attended, w_out, preferred_element_type=jnp.float32).astype(jnp.bfloat16)
+    projected = lax.psum_scatter(part, "seq", scatter_dimension=0, tiled=True)
+    projected = projected.astype(jnp.float32).reshape(seqs, local, width)
+    return (base + gate[:, None, :] * projected).astype(jnp.bfloat16)
+
+
 def solution(mesh):
+    n = mesh.shape["seq"]
+    body = functools.partial(head_split, n) if H % n == 0 else gathered
     placed = (
         P("group", "seq", None),
         P("group", "seq", None),
@@ -86,5 +130,5 @@
         P("seq", None),
     )
     return jax.shard_map(
-        per_device, mesh=mesh, in_specs=placed, out_specs=P("group", "seq", None), check_vma=False
+        body, mesh=mesh, in_specs=placed, out_specs=P("group", "seq", None), check_vma=False
     )

time: 282 us -> 243 us (0.86)
  waiting for transfers between devices: 185 us -> 128 us
  blocking collectives: 30 us -> 70.1 us
  local copies, waits for them, and re-layouts: 19.7 us -> 8.46 us
  starting transfers between devices: 9.72 us -> 0.09 us
  matrix products: 18.3 us -> 11.7 us
  other arithmetic: 4.83 us -> 10.7 us
    all_gather x3 -> x1, waiting for transfers between devices: 165 us -> 0.02 us  [head_split(): lax.all_gather(normed.reshape(rows, width), 'seq', axis=0, tiled=True)]
    reduce_scatter x0 -> x2, waiting for transfers between devices: none -> 128 us  [the longest x1 64.2 us: head_split(): merged = lax.psum_scatter(part, 'seq', scatter_dimension=0, tiled=True)]
    all_to_all x2, blocking collectives: 30 us -> 70.1 us  [the longest x1 48.7 us: head_split(): wq = lax.all_to_all(wq, 'seq', split_axis=2, concat_axis=0, tiled=True)]
    all_to_all x2 -> x0, waiting for transfers between devices: 18.2 us -> none  [the longest x1 9.96 us: per_device(): lax.all_to_all(value, 'seq', split_axis=0, concat_axis=1, tiled=True)]
    dot_general x2 -> x0, local copies, waits for them, and re-layouts: 16.5 us -> none  [the longest x1 16.3 us: per_device(): qkv = jnp.dot(normed, full_qkv, preferred_element_type=jnp.float32)]
    all_to_all x2 -> x0, starting transfers between devices: 9.64 us -> none  [the longest x1 5.45 us: per_device(): lax.all_to_all(key, 'seq', split_axis=0, concat_axis=1, tiled=True)]
    dot_general x12 -> x6, matrix products: 18.3 us -> 11.7 us  [the longest x1 3.56 us: head_split(): qkv = jnp.dot(every, wq, preferred_element_type=jnp.float32)]
    reshape x0 -> x3, local copies, waits for them, and re-layouts: none -> 5.77 us  [the longest x2 3.53 us: head_split(): wq = w_qkv.reshape(w_qkv.shape[0], 3, n, heads * HD)]
  transfers between devices with their start and end apart: 5 -> 3, of which waited for: 4 -> 2; matrix products, arithmetic and copies ran while one was open for 14% -> 3% of each run, Pallas kernels for 0% -> 0%
where the time goes in v1:
time: 243 us; the launch traced here: 242 us
  waiting for transfers between devices  128 us (53%)
  blocking collectives  70.1 us (29%)
  between operations  13.3 us (5%)
  matrix products  11.7 us (5%)
  other arithmetic  10.7 us (4%)
  local copies, waits for them, and re-layouts  8.46 us (3%)
    reduce_scatter x1, waiting for transfers between devices, head_split(): merged = lax.psum_scatter(part, 'seq', scatter_dimension=0, tiled=True)  64.2 us
    reduce_scatter x1, waiting for transfers between devices, head_split(): projected = lax.psum_scatter(part, 'seq', scatter_dimension=0, tiled=True)  63.5 us
    all_to_all x1, blocking collectives, head_split(): wq = lax.all_to_all(wq, 'seq', split_axis=2, concat_axis=0, tiled=True)  48.7 us
    all_to_all x1, blocking collectives, head_split(): lax.all_to_all(combined, 'seq', split_axis=1, concat_axis=0, tiled=True)  21.5 us
  transfers between devices with their start and end apart: 3, of which 2 were waited for; matrix products, arithmetic and copies ran while one was open for 3% of the time, Pallas kernels for 0%

profile of v1, /device:TPU:0, one launch (start us, length us, event | category | flops | bytes accessed | tf_op | source)
XLA Modules:
  0.0 242.1 jit_solution(9036021175794502180)
XLA Ops:
  6.5 1.2 pad_maximum_fusion
  7.7 1.0 all_to_all.25
  8.9 21.5 %all_to_all.34 = bf16[64,16,176]{2,0,1:T(8,128)(2,1)S(1)} all-to-all(bf16[64,16,176]{2,0,1:T(8,128)(2,1)S(1)} %copy.35), channel_id=1, replica_groups=mesh['group'=2,'seq'=16] {'seq'}, dimensions={1} | all-to-all | bytes 720896 | tf_op jit(solution)/shard_map/all_to_all | solution.py:93
  30.4 2.6 %convolution_convert_fusion.1 = bf16[1024,1408]{1,0:T(8,128)(2,1)} fusion(bf16[1024,176]{1,0:T(8,128)(2,1)S(1)} %bitcast.98, bf16[176,1408]{1,0:T(8,128)(2,1)S(1)} %copy-done.2), kind=kOutput, calls=%fused_computation.5 | convolution fusion | flops 508952576 | bytes 3739648 | tf_op jit(solution)/shard_map/dot_general | solution.py:97
  33.2 0.4 fusion.25
  33.6 64.2 %reduce-scatter.3.cloned.1.call-done = bf16[64,1408]{1,0:T(8,128)(2,1)} async-done(((bf16[1024,1408]{1,0:T(8,128)(2,1)}), bf16[64,1408]{1,0:T(8,128)(2,1)}) %reduce-scatter.3.cloned.1.call-update) | async-done | bytes 180240 | tf_op jit(solution)/shard_map/reduce_scatter | solution.py:98
  97.8 1.0 convert_reduce_fusion
  98.9 1.1 multiply_reduce_fusion
  100.0 1.7 fusion.16
  101.8 3.3 %reshape.188 = bf16[88,3,16,88]{3,2,1,0:T(8,128)(2,1)S(1)} reshape(bf16[88,4224]{1,0:T(8,128)(2,1)} %param.12) | data formatting | bytes 1486848 | tf_op jit(solution)/shard_map/reshape | solution.py:94
  105.1 0.3 copy.36
  105.4 48.7 %all_to_all.35 = bf16[88,3,16,88]{3,0,1,2:T(8,128)(2,1)S(1)} all-to-all(bf16[88,3,16,88]{3,0,1,2:T(8,128)(2,1)S(1)} %copy.36), channel_id=1, replica_groups=mesh['group'=2,'seq'=16] {'seq'}, dimensions={2} | all-to-all | bytes 1486848 | tf_op jit(solution)/shard_map/all_to_all | solution.py:95
  154.0 1.5 copy.37
  155.5 2.2 reshape.189
  157.8 3.6 %convolution_bitcast_fusion = f32[16,4,16,3,1,88]{5,2,3,1,0,4:T(8,128)S(1)} fusion(bf16[16,4,16,1408,1]{3,2,4,1,0:T(8,128)(2,1)} %bitcast.102, bf16[3,88,1408,1,1]{2,1,0,4,3:T(8,128)(2,1)S(1)} %bitcast.100), kind=kOutput, calls=%fused_computation.6 | convolution fusion | flops 761266176 | bytes 4708352 | tf_op jit(solution)/shard_map/dot_general | solution.py:104
  161.4 0.4 slice_reduce_fusion.1
  161.8 0.7 fusion.10
  162.6 0.6 fusion.17
  163.2 1.3 fusion.31
  164.5 2.0 fusion
  166.5 1.5 fusion.4
  168.0 2.5 %convolution_convert_fusion = bf16[1024,1408]{1,0:T(8,128)(2,1)} fusion(bf16[1024,88]{1,0:T(8,128)(2,1)S(1)} %bitcast.99, bf16[88,1408]{1,0:T(8,128)(2,1)S(1)} %copy-done.3), kind=kOutput, calls=%fused_computation.4 | convolution fusion | flops 255197184 | bytes 3311616 | tf_op jit(solution)/shard_map/dot_general | solution.py:114
  170.5 63.5 %reduce-scatter.5.cloned.1.call-done = bf16[64,1408]{1,0:T(8,128)(2,1)} async-done(((bf16[1024,1408]{1,0:T(8,128)(2,1)}), bf16[64,1408]{1,0:T(8,128)(2,1)}) %reduce-scatter.5.cloned.1.call-update) | async-done | bytes 180240 | tf_op jit(solution)/shard_map/reduce_scatter | solution.py:115
  234.0 1.6 fusion.15
  (28 shorter events, 0.6 us)
Async XLA Ops:
  6.5 26.6 %copy-start = (bf16[256,4224]{1,0:T(8,128)(2,1)S(1)}, bf16[256,4224]{1,0:T(8,128)(2,1)}, u32[]{:S(2)}) copy-start(bf16[256,4224]{1,0:T(8,128)(2,1)} %param.11) | copy-start | bytes 6488068
  6.5 23.8 %copy-start.2 = (bf16[176,1408]{1,0:T(8,128)(2,1)S(1)}, bf16[176,1408]{1,0:T(8,128)(2,1)}, u32[]{:S(2)}) copy-start(bf16[176,1408]{1,0:T(8,128)(2,1)} %param.10) | copy-start | bytes 1486852
  6.5 91.3 %reduce-scatter.3.cloned.1.call-start = ((), (), s32[]{:S(2)}) async-start(), calls=%async_computation.4 | async-start | bytes 3063808 | tf_op jit(solution)/shard_map/reduce_scatter | solution.py:98
  30.4 2.6 %copy-start.4 = (s32[4]{0:T(128)S(1)}, s32[4]{0:T(128)}, u32[]{:S(2)}) copy-start(s32[4]{0:T(128)} %param.9) | copy-start | bytes 52
  33.0 124.8 %all-gather.2.cloned.1.call-start = ((), (), s32[]{:S(2)}) async-start(), calls=%async_computation.5 | async-start | bytes 3063808 | tf_op jit(solution)/shard_map/all_gather | solution.py:103
  101.8 132.2 %reduce-scatter.5.cloned.1.call-start = ((), (), s32[]{:S(2)}) async-start(), calls=%async_computation.6 | async-start | bytes 3063808 | tf_op jit(solution)/shard_map/reduce_scatter | solution.py:115
  166.5 1.5 copy-start.3
  168.0 66.0 %copy-start.1 = (bf16[64,1408]{1,0:T(8,128)(2,1)S(1)}, bf16[64,1408]{1,0:T(8,128)(2,1)}, u32[]{:S(2)}) copy-start(bf16[64,1408]{1,0:T(8,128)(2,1)} %reduce-scatter.3.cloned.1.call-done) | copy-start | bytes 540676
Sparse Core Ops, SparseCore 0:
  33.1 64.6 reduce-scatter.2
  101.9 52.4 all-gather.1
  170.6 63.3 reduce-scatter.4
